TPU v7x, 32 devices: a whole 2x2x4 slice. The times are simulated.
32 devices in a mesh: dp: 2 (over x), expert: 16 (over z, y, core).
Axes of the slice: x: 2, y: 2, z: 4, core: 2. Of those that a mesh axis runs over, the one named last changes fastest.
Arguments:
- tokens: bfloat16 [2048, 2560], P('expert', 'dp'), may hold values from -6 to 6
- cotangent: bfloat16 [2048, 2560], P('expert', 'dp'), may hold values from -6 to 6
- expert_ids: int32 [2048, 6], P('expert'), may hold values from 0 to 15, all different within a row; in each aligned block of 128 rows (0 to 127, 128 to 255, ...) at most 64 rows name the same one
- gate_weights: float32 [2048, 6], P('expert'), may hold values from 0.1 to 0.6
- w_in: bfloat16 [16, 2560, 768], P('expert', 'dp'), may hold values from -0.125 to 0.125
- w_out: bfloat16 [16, 768, 2560], P('expert', None, 'dp'), may hold values from -0.21875 to 0.21875
Outputs:
- mixed_out: bfloat16 [2048, 2560], P('expert', 'dp')
- token_grad: bfloat16 [2048, 2560], P('expert', 'dp')
- w_in_grad: bfloat16 [16, 2560, 768], P('expert', 'dp')
- w_out_grad: bfloat16 [16, 768, 2560], P('expert', None, 'dp')
Inputs may be any that keep to these rules, and one draw needn't show every extreme that they name: `expert_ids`: each row names 6 different experts. Within the rows of one device (aligned blocks of 128 rows) no expert is named more than 64 times, a bound that some block reaches.
All inputs are finite; a program needn't handle non-finite values.
Results may differ from a plain program's by a relative error of at most 0.017.
Values may be sent and summed in bfloat16 or wider, within the bound.
A program may use at most 64 MiB of HBM per device.

v0:
```python
import jax
import jax.numpy as jnp
from jax import lax
from jax.sharding import PartitionSpec as P


def silu_slope(hidden_value):
    logistic = jax.nn.sigmoid(hidden_value)
    return logistic * (1.0 + hidden_value * (1.0 - logistic))


def expert_hidden(rows_x, weight_in):
    partial_sum = jnp.dot(rows_x, weight_in, preferred_element_type=jnp.float32)
    share_sum = lax.psum_scatter(
        partial_sum.astype(jnp.bfloat16), "dp", scatter_dimension=1, tiled=True
    ).astype(jnp.float32)
    share_act = jax.nn.silu(share_sum).astype(jnp.bfloat16)
    return (share_sum, lax.all_gather(share_act, "dp", axis=1, tiled=True))


def expert_slope(rows_dy, weight_out, preact):
    partial_sum = lax.dot_general(
        rows_dy, weight_out, (((1,), (1,)), ((), ())), preferred_element_type=jnp.float32
    )
    share_sum = lax.psum_scatter(
        partial_sum.astype(jnp.bfloat16), "dp", scatter_dimension=1, tiled=True
    ).astype(jnp.float32)
    share_delta = (share_sum * silu_slope(preact)).astype(jnp.bfloat16)
    return lax.all_gather(share_delta, "dp", axis=1, tiled=True)


def local(tokens, cotangent, expert_ids, gate_weights, w_in, w_out):
    experts = lax.axis_size("expert")
    tok_rows, quarter = tokens.shape
    choose_count = expert_ids.shape[1]
    capacity = max(2, 4 * tok_rows * choose_count // (3 * experts))
    assign = tok_rows * choose_count
    flat_ids = expert_ids.reshape(-1)
    onehot = (flat_ids[:, None] == jnp.arange(experts, dtype=jnp.int32)[None, :]).astype(jnp.int32)
    earlier = jnp.sum((jnp.cumsum(onehot, axis=0) - onehot) * onehot, axis=1)
    slot_index = flat_ids * capacity + earlier
    source = (
        jnp.full((experts * capacity,), assign, jnp.int32)
        .at[slot_index]
        .set(jnp.arange(assign, dtype=jnp.int32))
    )
    token_of = source // choose_count
    zero_row = jnp.zeros((1, quarter), jnp.bfloat16)
    send_x = jnp.concatenate([tokens, zero_row], 0)[token_of].reshape(experts, capacity, quarter)
    slot_gate = jnp.concatenate([gate_weights.reshape(-1), jnp.zeros((1,), jnp.float32)], 0)[source]
    picked_dy = jnp.concatenate([cotangent, zero_row], 0)[token_of]
    send_dy = (
        (slot_gate[:, None] * picked_dy.astype(jnp.float32))
        .astype(jnp.bfloat16)
        .reshape(experts, capacity, quarter)
    )
    weight_in = w_in[0]
    weight_out = w_out[0]
    arrived_x = lax.all_to_all(send_x, "expert", split_axis=0, concat_axis=0, tiled=True)
    rows_x = arrived_x.reshape(-1, quarter)
    preact, activation = expert_hidden(rows_x, weight_in)
    out_rows = jnp.dot(activation, weight_out, preferred_element_type=jnp.float32).astype(
        jnp.bfloat16
    )
    rows_x, preact, activation, out_rows = (
        rows_x,
        preact,
        activation,
        out_rows.reshape(experts, capacity, quarter),
    )
    returned_out = lax.all_to_all(out_rows, "expert", split_axis=0, concat_axis=0, tiled=True)
    arrived_dy = lax.all_to_all(send_dy, "expert", split_axis=0, concat_axis=0, tiled=True)
    rows_dy = arrived_dy.reshape(-1, quarter)
    delta_hidden = expert_slope(rows_dy, weight_out, preact)
    out_grad = lax.dot_general(
        activation, rows_dy, (((0,), (0,)), ((), ())), preferred_element_type=jnp.float32
    ).astype(jnp.bfloat16)
    in_grad = lax.dot_general(
        rows_x, delta_hidden, (((0,), (0,)), ((), ())), preferred_element_type=jnp.float32
    ).astype(jnp.bfloat16)
    back_rows = lax.dot_general(
        delta_hidden, weight_in, (((1,), (1,)), ((), ())), preferred_element_type=jnp.float32
    ).astype(jnp.bfloat16)
    in_grad, out_grad, back_rows = (
        in_grad[None],
        out_grad[None],
        back_rows.reshape(experts, capacity, quarter),
    )
    returned_back = lax.all_to_all(back_rows, "expert", split_axis=0, concat_axis=0, tiled=True)

    def gather_rows(returned):
        flat_rows = returned.reshape(experts * capacity, quarter)
        return flat_rows[slot_index].astype(jnp.float32).reshape(tok_rows, choose_count, quarter)

    mixed_out = jnp.sum(gather_rows(returned_out) * gate_weights[:, :, None], axis=1).astype(
        jnp.bfloat16
    )
    token_grad = jnp.sum(gather_rows(returned_back), axis=1).astype(jnp.bfloat16)
    return (mixed_out, token_grad, in_grad, out_grad)


def solution(mesh):
    in_specs = (
        P("expert", "dp"),
        P("expert", "dp"),
        P("expert", None),
        P("expert", None),
        P("expert", "dp", None),
        P("expert", None, "dp"),
    )
    out_specs = (
        P("expert", "dp"),
        P("expert", "dp"),
        P("expert", "dp", None),
        P("expert", None, "dp"),
    )
    return jax.shard_map(local, mesh=mesh, in_specs=in_specs, out_specs=out_specs, check_vma=False)
```

profile of v0, /device:TPU:13, one launch (start us, length us, event | category | flops | bytes accessed | tf_op | source)
XLA Modules:
  0.0 386.5 jit_solution(10710059806611601516)
XLA Ops:
  15.9 4.5 %gather_fusion.2 = f32[1024]{0:T(1024)S(1)} fusion(f32[769]{0:T(1024)S(1)} %pad_maximum_fusion, s32[1024]{0:T(1024)S(1)} %get-tuple-element.6), kind=kCustom, calls=%fused_computation.2 | custom fusion | bytes 12288 | tf_op jit(solution)/shard_map/gather | solution.py:50
  20.5 5.5 %gather_fusion.3 = bf16[1024,1280]{1,0:T(8,128)(2,1)} fusion(bf16[129,1280]{1,0:T(8,128)(2,1)S(1)} %concatenate.11, s32[1024]{0:T(1024)S(1)} %get-tuple-element.7), kind=kCustom, calls=%fused_computation.3 | custom fusion | bytes 5246976 | tf_op jit(solution)/shard_map/gather | solution.py:51
  29.8 6.7 %all-to-all-start.2 = ((bf16[16,64,1280]{2,1,0:T(8,128)(2,1)}), bf16[16,64,1280]{2,1,0:T(8,128)(2,1)}, u32[]{:S(2)}, u32[]{:S(2)}) async-start(bf16[16,64,1280]{2,1,0:T(8,128)(2,1)} %fusion), calls=%async_computation.2 | async-start | bytes 5242880 | tf_op jit(solution)/shard_map/all_to_all | solution.py:72
  36.4 5.5 %gather_fusion = bf16[1024,1280]{1,0:T(8,128)(2,1)} fusion(bf16[129,1280]{1,0:T(8,128)(2,1)S(1)} %concatenate.9, s32[1024]{0:T(1024)S(1)} %get-tuple-element.7), kind=kCustom, calls=%fused_computation | custom fusion | bytes 5246976 | tf_op jit(solution)/shard_map/gather | solution.py:49
  41.9 53.3 %all-to-all-done.2 = bf16[16,64,1280]{2,1,0:T(8,128)(2,1)} async-done(((bf16[16,64,1280]{2,1,0:T(8,128)(2,1)}), bf16[16,64,1280]{2,1,0:T(8,128)(2,1)}, u32[]{:S(2)}, u32[]{:S(2)}) %all-to-all-start.2) | async-done | bytes 2621472 | tf_op jit(solution)/shard_map/all_to_all | solution.py:72
  95.2 4.8 %all-to-all-start = ((bf16[16,64,1280]{2,1,0:T(8,128)(2,1)}), bf16[16,64,1280]{2,1,0:T(8,128)(2,1)}, u32[]{:S(2)}, u32[]{:S(2)}) async-start(bf16[16,64,1280]{2,1,0:T(8,128)(2,1)} %bitcast.60), calls=%async_computation | async-start | bytes 5242880 | tf_op jit(solution)/shard_map/all_to_all | solution.py:59
  105.7 53.0 %all-to-all-done = bf16[16,64,1280]{2,1,0:T(8,128)(2,1)} async-done(((bf16[16,64,1280]{2,1,0:T(8,128)(2,1)}), bf16[16,64,1280]{2,1,0:T(8,128)(2,1)}, u32[]{:S(2)}, u32[]{:S(2)}) %all-to-all-start) | async-done | bytes 2621472 | tf_op jit(solution)/shard_map/all_to_all | solution.py:59
  158.7 4.5 %fusion.9 = bf16[1024,768]{1,0:T(8,128)(2,1)S(1)} fusion(bf16[1024,1280]{1,0:T(8,128)(2,1)} %bitcast.2, bf16[1,1280,768]{2,1,0:T(8,128)(2,1)} %param.10), kind=kOutput, calls=%fused_computation.24 | convolution fusion | flops 2014052352 | bytes 6160384 | tf_op jit(solution)/shard_map/dot_general | solution.py:13
  166.5 24.0 %reduce-scatter.7.cloned.1.call-done = bf16[384,1024]{1,0:T(8,128)(2,1)} async-done(((bf16[768,1024]{1,0:T(8,128)(2,1)}), bf16[384,1024]{1,0:T(8,128)(2,1)}) %reduce-scatter.7.cloned.1.call-update) | async-done | bytes 786448
  193.8 27.4 %all-gather.3.cloned.1.call-done = bf16[1024,768]{1,0:T(8,128)(2,1)} async-done(((bf16[1024,384]{1,0:T(8,128)(2,1)}), bf16[1024,768]{1,0:T(8,128)(2,1)}) %all-gather.3.cloned.1.call-update) | async-done | bytes 1572880 | tf_op jit(solution)/shard_map/all_gather | solution.py:18
  221.2 5.2 %convolution_convert_fusion.1 = bf16[1024,1280]{1,0:T(8,128)(2,1)} fusion(bf16[1024,768]{1,0:T(8,128)(2,1)} %all-gather.3.cloned.1.call-done, bf16[1,768,1280]{2,1,0:T(8,128)(2,1)S(1)} %copy-done), kind=kOutput, calls=%fused_computation.10 | convolution fusion | flops 2014576640 | bytes 6160384 | tf_op jit(solution)/shard_map/dot_general | solution.py:62
  226.4 6.5 %all-to-all-start.1 = ((bf16[16,64,1280]{2,1,0:T(8,128)(2,1)}), bf16[16,64,1280]{2,1,0:T(8,128)(2,1)}, u32[]{:S(2)}, u32[]{:S(2)}) async-start(bf16[16,64,1280]{2,1,0:T(8,128)(2,1)} %bitcast.64), calls=%async_computation.1 | async-start | bytes 5242880 | tf_op jit(solution)/shard_map/all_to_all | solution.py:71
  233.4 28.8 %all-gather.5.cloned.1.call-done = bf16[1024,768]{1,0:T(8,128)(2,1)} async-done(((bf16[1024,384]{1,0:T(8,128)(2,1)}), bf16[1024,768]{1,0:T(8,128)(2,1)}) %all-gather.5.cloned.1.call-update) | async-done | bytes 1572880 | tf_op jit(solution)/shard_map/all_gather | solution.py:29
  262.2 5.8 %convolution_convert_fusion = bf16[1024,1280]{1,0:T(8,128)(2,1)} fusion(bf16[1024,768]{1,0:T(8,128)(2,1)} %all-gather.5.cloned.1.call-done, bf16[1,1280,768]{2,1,0:T(8,128)(2,1)} %param.10), kind=kOutput, calls=%fused_computation.9 | convolution fusion | flops 2014576640 | bytes 6160384 | tf_op jit(solution)/shard_map/dot_general | solution.py:81
  268.0 23.6 %all-to-all-done.1 = bf16[16,64,1280]{2,1,0:T(8,128)(2,1)} async-done(((bf16[16,64,1280]{2,1,0:T(8,128)(2,1)}), bf16[16,64,1280]{2,1,0:T(8,128)(2,1)}, u32[]{:S(2)}, u32[]{:S(2)}) %all-to-all-start.1) | async-done | bytes 2621472 | tf_op jit(solution)/shard_map/all_to_all | solution.py:71
  291.6 4.8 %all-to-all-start.3 = ((bf16[16,64,1280]{2,1,0:T(8,128)(2,1)}), bf16[16,64,1280]{2,1,0:T(8,128)(2,1)}, u32[]{:S(2)}, u32[]{:S(2)}) async-start(bf16[16,64,1280]{2,1,0:T(8,128)(2,1)} %bitcast.65), calls=%async_computation.3 | async-start | bytes 5242880 | tf_op jit(solution)/shard_map/all_to_all | solution.py:89
  296.4 5.9 %fusion.1 = bf16[1,1280,768]{2,1,0:T(8,128)(2,1)} fusion(bf16[1024,1280]{1,0:T(8,128)(2,1)} %bitcast.2, bf16[1024,768]{1,0:T(8,128)(2,1)} %all-gather.5.cloned.1.call-done), kind=kOutput, calls=%fused_computation.13 | convolution fusion | flops 2014248960 | bytes 6160384 | tf_op jit(solution)/shard_map/dot_general | solution.py:78
  302.3 5.3 %fusion.2 = bf16[1,768,1280]{2,1,0:T(8,128)(2,1)} fusion(bf16[1024,768]{1,0:T(8,128)(2,1)S(1)} %copy-done.5, bf16[1024,1280]{1,0:T(8,128)(2,1)} %bitcast.8), kind=kOutput, calls=%fused_computation.14 | convolution fusion | flops 2014248960 | bytes 6160384 | tf_op jit(solution)/shard_map/dot_general | solution.py:75
  307.5 7.3 %gather_fusion.1 = bf16[768,1280]{1,0:T(8,128)(2,1)} fusion(bf16[1024,1280]{1,0:T(8,128)(2,1)} %bitcast.6, s32[1024]{0:T(1024)S(1)} %pad_clamp_fusion), kind=kCustom, calls=%fused_computation.1 | custom fusion | bytes 3935232 | tf_op jit(solution)/shard_map/gather | solution.py:93
  314.8 40.3 %all-to-all-done.3 = bf16[16,64,1280]{2,1,0:T(8,128)(2,1)} async-done(((bf16[16,64,1280]{2,1,0:T(8,128)(2,1)}), bf16[16,64,1280]{2,1,0:T(8,128)(2,1)}, u32[]{:S(2)}, u32[]{:S(2)}) %all-to-all-start.3) | async-done | bytes 2621472 | tf_op jit(solution)/shard_map/all_to_all | solution.py:89
  355.2 7.3 %gather_fusion.4 = bf16[768,1280]{1,0:T(8,128)(2,1)} fusion(bf16[1024,1280]{1,0:T(8,128)(2,1)} %bitcast.10, s32[1024]{0:T(1024)S(1)} %pad_clamp_fusion), kind=kCustom, calls=%fused_computation.4 | custom fusion | bytes 3935232 | tf_op jit(solution)/shard_map/gather | solution.py:93
  362.4 4.1 %gather.22 = bf16[128,6,1280]{2,1,0:T(8,128)(2,1)} reshape(bf16[768,1280]{1,0:T(8,128)(2,1)} %gather_fusion.4) | data formatting | bytes 3932160 | tf_op jit(solution)/shard_map/gather | solution.py:93
  370.6 4.5 %reshape.104 = f32[128,6,1280]{2,1,0:T(8,128)} reshape(bf16[768,1280]{1,0:T(8,128)(2,1)} %gather_fusion.1) | data formatting | bytes 5898240 | tf_op jit(solution)/shard_map/convert_element_type | solution.py:93
  375.1 4.9 %multiply_reduce_fusion = bf16[128,1280]{1,0:T(8,128)(2,1)} fusion(f32[128,6,1280]{2,1,0:T(8,128)} %reshape.104, f32[128,6]{1,0:T(8,128)S(1)} %copy-done.2), kind=kLoop, calls=%fused_computation.8 | loop fusion | flops 1802240 | bytes 4262912 | tf_op jit(solution)/shard_map/reduce_sum | solution.py:95
  (51 shorter events, 29.4 us)
Async XLA Ops:
  7.2 92.8 %copy-start = (bf16[1,768,1280]{2,1,0:T(8,128)(2,1)S(1)}, bf16[1,768,1280]{2,1,0:T(8,128)(2,1)}, u32[]{:S(2)}) copy-start(bf16[1,768,1280]{2,1,0:T(8,128)(2,1)} %param.11) | copy-start | bytes 5898244
  10.1 5.7 %copy-start.1 = (f32[128,6]{1,0:T(8,128)}, f32[128,6]{1,0:T(8,128)S(1)}, u32[]{:S(2)}) copy-start(f32[128,6]{1,0:T(8,128)S(1)} %copy.21) | copy-start | bytes 9220
  15.9 4.6 %copy-start.3 = (bf16[128,1280]{1,0:T(8,128)(2,1)S(1)}, bf16[128,1280]{1,0:T(8,128)(2,1)}, u32[]{:S(2)}) copy-start(bf16[128,1280]{1,0:T(8,128)(2,1)} %param.7) | copy-start | bytes 983044
  29.7 6.7 %copy-start.4 = (bf16[128,1280]{1,0:T(8,128)(2,1)S(1)}, bf16[128,1280]{1,0:T(8,128)(2,1)}, u32[]{:S(2)}) copy-start(bf16[128,1280]{1,0:T(8,128)(2,1)} %param.6) | copy-start | bytes 983044
  29.8 65.4 %all-to-all-start.2 = ((bf16[16,64,1280]{2,1,0:T(8,128)(2,1)}), bf16[16,64,1280]{2,1,0:T(8,128)(2,1)}, u32[]{:S(2)}, u32[]{:S(2)}) async-start(bf16[16,64,1280]{2,1,0:T(8,128)(2,1)} %fusion), calls=%async_computation.2 | async-start | bytes 5242880 | tf_op jit(solution)/shard_map/all_to_all | solution.py:72
  95.2 63.5 %all-to-all-start = ((bf16[16,64,1280]{2,1,0:T(8,128)(2,1)}), bf16[16,64,1280]{2,1,0:T(8,128)(2,1)}, u32[]{:S(2)}, u32[]{:S(2)}) async-start(bf16[16,64,1280]{2,1,0:T(8,128)(2,1)} %bitcast.60), calls=%async_computation | async-start | bytes 5242880 | tf_op jit(solution)/shard_map/all_to_all | solution.py:59
  99.9 65.0 %reduce-scatter.9.cloned.1.call-start = ((), (), s32[]{:S(2)}) async-start(), calls=%async_computation.9 | async-start | bytes 2359296
  105.6 84.8 %reduce-scatter.7.cloned.1.call-start = ((), (), s32[]{:S(2)}) async-start(), calls=%async_computation.8 | async-start | bytes 2359296
  164.9 56.3 %all-gather.3.cloned.1.call-start = ((), (), s32[]{:S(2)}) async-start(), calls=%async_computation.6 | async-start | bytes 2359296 | tf_op jit(solution)/shard_map/all_gather | solution.py:18
  226.4 65.3 %all-to-all-start.1 = ((bf16[16,64,1280]{2,1,0:T(8,128)(2,1)}), bf16[16,64,1280]{2,1,0:T(8,128)(2,1)}, u32[]{:S(2)}, u32[]{:S(2)}) async-start(bf16[16,64,1280]{2,1,0:T(8,128)(2,1)} %bitcast.64), calls=%async_computation.1 | async-start | bytes 5242880 | tf_op jit(solution)/shard_map/all_to_all | solution.py:71
  232.9 29.3 %all-gather.5.cloned.1.call-start = ((), (), s32[]{:S(2)}) async-start(), calls=%async_computation.7 | async-start | bytes 2359296 | tf_op jit(solution)/shard_map/all_gather | solution.py:29
  291.6 63.5 %all-to-all-start.3 = ((bf16[16,64,1280]{2,1,0:T(8,128)(2,1)}), bf16[16,64,1280]{2,1,0:T(8,128)(2,1)}, u32[]{:S(2)}, u32[]{:S(2)}) async-start(bf16[16,64,1280]{2,1,0:T(8,128)(2,1)} %bitcast.65), calls=%async_computation.3 | async-start | bytes 5242880 | tf_op jit(solution)/shard_map/all_to_all | solution.py:89
  296.4 5.9 %copy-start.5 = (bf16[1024,768]{1,0:T(8,128)(2,1)S(1)}, bf16[1024,768]{1,0:T(8,128)(2,1)}, u32[]{:S(2)}) copy-start(bf16[1024,768]{1,0:T(8,128)(2,1)} %all-gather.3.cloned.1.call-done) | copy-start | bytes 4718596
  370.6 4.5 %copy-start.2 = (f32[128,6]{1,0:T(8,128)S(1)}, f32[128,6]{1,0:T(8,128)}, u32[]{:S(2)}) copy-start(f32[128,6]{1,0:T(8,128)} %copy-done.1) | copy-start | bytes 9220
Sparse Core Ops, SparseCore 0:
  105.7 26.5 reduce-scatter.8
  165.0 25.3 reduce-scatter.6
  194.0 27.1 all-gather.2
  235.5 26.6 all-gather.4
where the time goes:
time: 387 us
  waiting for transfers between devices  251 us (65%)
  local copies, waits for them, and re-layouts  50.9 us (13%)
  matrix products  30.5 us (8%)
  starting transfers between devices  22.9 us (6%)
  other arithmetic  17.3 us (4%)
  between operations  14 us (4%)
    all_to_all x1, waiting for transfers between devices, local(): lax.all_to_all(send_dy, 'expert', split_axis=0, concat_axis=0, tiled=True)  53.3 us
    all_to_all x1, waiting for transfers between devices, local(): lax.all_to_all(send_x, 'expert', split_axis=0, concat_axis=0, tiled=True)  53 us
    all_to_all x1, waiting for transfers between devices, local(): lax.all_to_all(back_rows, 'expert', split_axis=0, concat_axis=0, tiled=True)  40.3 us
    all_gather x1, waiting for transfers between devices, expert_slope(): return lax.all_gather(share_delta, 'dp', axis=1, tiled=True)  28.8 us
    all_gather x1, waiting for transfers between devices, expert_hidden(): return (share_sum, lax.all_gather(share_act, 'dp', axis=1, tiled=True))  27.4 us
    unnamed x6, waiting for transfers between devices  24.6 us
    all_to_all x1, waiting for transfers between devices, local(): lax.all_to_all(out_rows, 'expert', split_axis=0, concat_axis=0, tiled=True)  23.6 us
    gather x3, local copies, waits for them, and re-layouts, gather_rows(): flat_rows[slot_index].astype(jnp.float32)  18.6 us
  transfers between devices with their start and end apart: 8, of which 7 were waited for; matrix products, arithmetic and copies ran while one was open for 11% of the time, Pallas kernels for 0%

commit v1 on v0

--- a/solution.py
+++ b/solution.py
@@ -56,7 +56,15 @@
     )
     weight_in = w_in[0]
     weight_out = w_out[0]
-    arrived_x = lax.all_to_all(send_x, "expert", split_axis=0, concat_axis=0, tiled=True)
+    ways, here = (lax.axis_size("expert"), lax.axis_index("expert"))
+    width = send_x.shape[0] // ways
+    turned = jnp.roll(send_x, -here * width, axis=0)
+    got = [lax.slice_in_dim(turned, 0, width, axis=0)]
+    for far in range(1, ways):
+        sent = lax.slice_in_dim(turned, far * width, (far + 1) * width, axis=0)
+        got.append(lax.ppermute(sent, "expert", [(d, (d + far) % ways) for d in range(ways)]))
+    line = jnp.concatenate(got[::-1], axis=0)
+    arrived_x = jnp.roll(line, (here + 1) * got[0].shape[0], axis=0)
     rows_x = arrived_x.reshape(-1, quarter)
     preact, activation = expert_hidden(rows_x, weight_in)
     out_rows = jnp.dot(activation, weight_out, preferred_element_type=jnp.float32).astype(

time: 387 us -> 450 us (1.16)
  waiting for transfers between devices: 251 us -> 286 us
  starting transfers between devices: 22.9 us -> 44.6 us
  local copies, waits for them, and re-layouts: 50.9 us -> 56.8 us
    ppermute x0 -> x15, waiting for transfers between devices: none -> 112 us  [local(): lax.ppermute(sent, 'expert', [(d, (d + far) % ways) for d in range(ways)])]
    all_to_all x1, waiting for transfers between devices: 53.3 us -> 0.01 us  [local(): lax.all_to_all(send_dy, 'expert', split_axis=0, concat_axis=0, tiled=True)]
    all_to_all x1 -> x0, waiting for transfers between devices: 53 us -> none  [local(): lax.all_to_all(send_x, 'expert', split_axis=0, concat_axis=0, tiled=True)]
    unnamed x6, waiting for transfers between devices: 24.6 us -> 50.8 us
    ppermute x0 -> x15, starting transfers between devices: none -> 24.5 us  [local(): lax.ppermute(sent, 'expert', [(d, (d + far) % ways) for d in range(ways)])]
    unnamed x18 -> x49, local copies, waits for them, and re-layouts: 7.84 us -> 15.6 us
    gather x3, local copies, waits for them, and re-layouts: 18.6 us -> 13.6 us  [gather_rows(): flat_rows[slot_index].astype(jnp.float32)]
    all_to_all x1 -> x0, starting transfers between devices: 4.78 us -> none  [local(): lax.all_to_all(send_x, 'expert', split_axis=0, concat_axis=0, tiled=True)]
  transfers between devices with their start and end apart: 8 -> 22, of which waited for: 7 -> 16; matrix products, arithmetic and copies ran while one was open for 11% -> 12% of each run, Pallas kernels for 0% -> 0%
where the time goes in v1:
time: 450 us; the launch traced here: 449 us
  waiting for transfers between devices  286 us (64%)
  local copies, waits for them, and re-layouts  56.8 us (13%)
  starting transfers between devices  44.6 us (10%)
  matrix products  28.2 us (6%)
  other arithmetic  19.2 us (4%)
  between operations  14.1 us (3%)
    ppermute x15, waiting for transfers between devices, local(): lax.ppermute(sent, 'expert', [(d, (d + far) % ways) for d in range(ways)])  112 us
    unnamed x6, waiting for transfers between devices  50.8 us
    all_to_all x1, waiting for transfers between devices, local(): lax.all_to_all(back_rows, 'expert', split_axis=0, concat_axis=0, tiled=True)  43.9 us
    all_gather x1, waiting for transfers between devices, expert_slope(): return lax.all_gather(share_delta, 'dp', axis=1, tiled=True)  28.8 us
    all_gather x1, waiting for transfers between devices, expert_hidden(): return (share_sum, lax.all_gather(share_act, 'dp', axis=1, tiled=True))  27.3 us
    ppermute x15, starting transfers between devices, local(): lax.ppermute(sent, 'expert', [(d, (d + far) % ways) for d in range(ways)])  24.5 us
    all_to_all x1, waiting for transfers between devices, local(): lax.all_to_all(out_rows, 'expert', split_axis=0, concat_axis=0, tiled=True)  23.5 us
    unnamed x49, local copies, waits for them, and re-layouts  15.6 us
  transfers between devices with their start and end apart: 22, of which 16 were waited for; matrix products, arithmetic and copies ran while one was open for 12% of the time, Pallas kernels for 0%

profile of v1, /device:TPU:13, one launch (start us, length us, event | category | flops | bytes accessed | tf_op | source)
XLA Modules:
  0.0 449.4 jit_solution(4815344646418998919)
XLA Ops:
  15.9 5.5 %gather_fusion = bf16[1024,1280]{1,0:T(8,128)(2,1)} fusion(bf16[129,1280]{1,0:T(8,128)(2,1)S(1)} %concatenate.15, s32[1024]{0:T(1024)S(1)} %get-tuple-element.23), kind=kCustom, calls=%fused_computation | custom fusion | bytes 5246976 | tf_op jit(solution)/shard_map/gather | solution.py:49
  33.0 5.5 %gather_fusion.3 = bf16[1024,1280]{1,0:T(8,128)(2,1)} fusion(bf16[129,1280]{1,0:T(8,128)(2,1)S(1)} %concatenate.18, s32[1024]{0:T(1024)S(1)} %get-tuple-element.23), kind=kCustom, calls=%fused_computation.3 | custom fusion | bytes 5246976 | tf_op jit(solution)/shard_map/gather | solution.py:51
  42.2 8.5 %all-to-all-start.1 = ((bf16[16,64,1280]{2,1,0:T(8,128)(2,1)}), bf16[16,64,1280]{2,1,0:T(8,128)(2,1)}, u32[]{:S(2)}, u32[]{:S(2)}) async-start(bf16[16,64,1280]{2,1,0:T(8,128)(2,1)} %fusion), calls=%async_computation.1 | async-start | bytes 5242880 | tf_op jit(solution)/shard_map/all_to_all | solution.py:80
  56.3 61.6 %collective-permute-done.1 = bf16[1,64,1280]{2,1,0:T(8,128)(2,1)S(1)} collective-permute-done((bf16[1,64,1280]{2,1,0:T(8,128)(2,1)}, bf16[1,64,1280]{2,1,0:T(8,128)(2,1)S(1)}, u32[]{:S(2)}, u32[]{:S(2)}) %collective-permute-start.1) | collective-permute-done | bytes 163872 | tf_op jit(solution)/shard_map/ppermute | solution.py:65
  117.9 5.8 %collective-permute-done.2 = bf16[1,64,1280]{2,1,0:T(8,128)(2,1)S(1)} collective-permute-done((bf16[1,64,1280]{2,1,0:T(8,128)(2,1)}, bf16[1,64,1280]{2,1,0:T(8,128)(2,1)S(1)}, u32[]{:S(2)}, u32[]{:S(2)}) %collective-permute-start.2) | collective-permute-done | bytes 163872 | tf_op jit(solution)/shard_map/ppermute | solution.py:65
  123.7 4.9 %collective-permute-done.3 = bf16[1,64,1280]{2,1,0:T(8,128)(2,1)S(1)} collective-permute-done((bf16[1,64,1280]{2,1,0:T(8,128)(2,1)}, bf16[1,64,1280]{2,1,0:T(8,128)(2,1)S(1)}, u32[]{:S(2)}, u32[]{:S(2)}) %collective-permute-start.3) | collective-permute-done | bytes 163872 | tf_op jit(solution)/shard_map/ppermute | solution.py:65
  130.4 5.9 %collective-permute-done.4 = bf16[1,64,1280]{2,1,0:T(8,128)(2,1)S(1)} collective-permute-done((bf16[1,64,1280]{2,1,0:T(8,128)(2,1)}, bf16[1,64,1280]{2,1,0:T(8,128)(2,1)S(1)}, u32[]{:S(2)}, u32[]{:S(2)}) %collective-permute-start.4) | collective-permute-done | bytes 163872 | tf_op jit(solution)/shard_map/ppermute | solution.py:65
  137.5 6.5 %collective-permute-done.5 = bf16[1,64,1280]{2,1,0:T(8,128)(2,1)S(1)} collective-permute-done((bf16[1,64,1280]{2,1,0:T(8,128)(2,1)}, bf16[1,64,1280]{2,1,0:T(8,128)(2,1)S(1)}, u32[]{:S(2)}, u32[]{:S(2)}) %collective-permute-start.5) | collective-permute-done | bytes 163872 | tf_op jit(solution)/shard_map/ppermute | solution.py:65
  144.0 6.5 %collective-permute-done.6 = bf16[1,64,1280]{2,1,0:T(8,128)(2,1)S(1)} collective-permute-done((bf16[1,64,1280]{2,1,0:T(8,128)(2,1)S(1)}, bf16[1,64,1280]{2,1,0:T(8,128)(2,1)S(1)}, u32[]{:S(2)}, u32[]{:S(2)}) %collective-permute-start.6) | collective-permute-done | bytes 163872 | tf_op jit(solution)/shard_map/ppermute | solution.py:65
  150.5 6.2 %collective-permute-start.7 = (bf16[1,64,1280]{2,1,0:T(8,128)(2,1)S(1)}, bf16[1,64,1280]{2,1,0:T(8,128)(2,1)S(1)}, u32[]{:S(2)}, u32[]{:S(2)}) collective-permute-start(bf16[1,64,1280]{2,1,0:T(8,128)(2,1)S(1)} %copy-done.9), channel_id=1, source_target_pairs={{0,8},{1,9},{2,10},{3,11},{4,12},{5,13},{6,14},{7,15},{8,0},{9,1},... | collective-permute-start | bytes 491528 | tf_op jit(solution)/shard_map/ppermute | solution.py:65
  156.8 6.2 %collective-permute-done.7 = bf16[1,64,1280]{2,1,0:T(8,128)(2,1)S(1)} collective-permute-done((bf16[1,64,1280]{2,1,0:T(8,128)(2,1)S(1)}, bf16[1,64,1280]{2,1,0:T(8,128)(2,1)S(1)}, u32[]{:S(2)}, u32[]{:S(2)}) %collective-permute-start.7) | collective-permute-done | bytes 163872 | tf_op jit(solution)/shard_map/ppermute | solution.py:65
  173.6 6.4 %collective-permute-done.9 = bf16[1,64,1280]{2,1,0:T(8,128)(2,1)S(1)} collective-permute-done((bf16[1,64,1280]{2,1,0:T(8,128)(2,1)S(1)}, bf16[1,64,1280]{2,1,0:T(8,128)(2,1)S(1)}, u32[]{:S(2)}, u32[]{:S(2)}) %collective-permute-start.9) | collective-permute-done | bytes 163872 | tf_op jit(solution)/shard_map/ppermute | solution.py:65
  204.9 22.7 %reduce-scatter.7.cloned.1.call-done = bf16[384,1024]{1,0:T(8,128)(2,1)} async-done(((bf16[768,1024]{1,0:T(8,128)(2,1)}), bf16[384,1024]{1,0:T(8,128)(2,1)}) %reduce-scatter.7.cloned.1.call-update) | async-done | bytes 786448
  229.0 27.5 %reduce-scatter.9.cloned.1.call-done = bf16[384,1024]{1,0:T(8,128)(2,1)} async-done(((bf16[768,1024]{1,0:T(8,128)(2,1)}), bf16[384,1024]{1,0:T(8,128)(2,1)}) %reduce-scatter.9.cloned.1.call-update) | async-done | bytes 786448
  259.9 27.3 %all-gather.3.cloned.1.call-done = bf16[1024,768]{1,0:T(8,128)(2,1)} async-done(((bf16[1024,384]{1,0:T(8,128)(2,1)}), bf16[1024,768]{1,0:T(8,128)(2,1)}) %all-gather.3.cloned.1.call-update) | async-done | bytes 1572880 | tf_op jit(solution)/shard_map/all_gather | solution.py:18
  287.3 5.1 %convolution_convert_fusion.1 = bf16[1024,1280]{1,0:T(8,128)(2,1)} fusion(bf16[1024,768]{1,0:T(8,128)(2,1)} %all-gather.3.cloned.1.call-done, bf16[1,768,1280]{2,1,0:T(8,128)(2,1)S(1)} %copy-done), kind=kOutput, calls=%fused_computation.14 | convolution fusion | flops 2014576640 | bytes 6160384 | tf_op jit(solution)/shard_map/dot_general | solution.py:70
  292.3 6.5 %all-to-all-start = ((bf16[16,64,1280]{2,1,0:T(8,128)(2,1)}), bf16[16,64,1280]{2,1,0:T(8,128)(2,1)S(1)}, u32[]{:S(2)}, u32[]{:S(2)}) async-start(bf16[16,64,1280]{2,1,0:T(8,128)(2,1)} %bitcast.65), calls=%async_computation | async-start | bytes 5242880 | tf_op jit(solution)/shard_map/all_to_all | solution.py:79
  299.4 28.8 %all-gather.5.cloned.1.call-done = bf16[1024,768]{1,0:T(8,128)(2,1)} async-done(((bf16[1024,384]{1,0:T(8,128)(2,1)}), bf16[1024,768]{1,0:T(8,128)(2,1)}) %all-gather.5.cloned.1.call-update) | async-done | bytes 1572880 | tf_op jit(solution)/shard_map/all_gather | solution.py:29
  328.2 5.8 %convolution_convert_fusion = bf16[1024,1280]{1,0:T(8,128)(2,1)} fusion(bf16[1024,768]{1,0:T(8,128)(2,1)} %all-gather.5.cloned.1.call-done, bf16[1,1280,768]{2,1,0:T(8,128)(2,1)} %param.12), kind=kOutput, calls=%fused_computation.13 | convolution fusion | flops 2014576640 | bytes 6160384 | tf_op jit(solution)/shard_map/dot_general | solution.py:89
  334.0 23.5 %all-to-all-done = bf16[16,64,1280]{2,1,0:T(8,128)(2,1)S(1)} async-done(((bf16[16,64,1280]{2,1,0:T(8,128)(2,1)}), bf16[16,64,1280]{2,1,0:T(8,128)(2,1)S(1)}, u32[]{:S(2)}, u32[]{:S(2)}) %all-to-all-start) | async-done | bytes 2621472 | tf_op jit(solution)/shard_map/all_to_all | solution.py:79
  362.3 5.9 %fusion.1 = bf16[1,1280,768]{2,1,0:T(8,128)(2,1)} fusion(bf16[1024,1280]{1,0:T(8,128)(2,1)} %bitcast.68, bf16[1024,768]{1,0:T(8,128)(2,1)} %all-gather.5.cloned.1.call-done), kind=kOutput, calls=%fused_computation.17 | convolution fusion | flops 2014248960 | bytes 6160384 | tf_op jit(solution)/shard_map/dot_general | solution.py:86
  368.2 5.3 %fusion.2 = bf16[1,768,1280]{2,1,0:T(8,128)(2,1)} fusion(bf16[1024,768]{1,0:T(8,128)(2,1)S(1)} %copy-done.13, bf16[1024,1280]{1,0:T(8,128)(2,1)} %bitcast.8), kind=kOutput, calls=%fused_computation.18 | convolution fusion | flops 2014248960 | bytes 6160384 | tf_op jit(solution)/shard_map/dot_general | solution.py:83
  377.1 43.9 %all-to-all-done.2 = bf16[16,64,1280]{2,1,0:T(8,128)(2,1)} async-done(((bf16[16,64,1280]{2,1,0:T(8,128)(2,1)}), bf16[16,64,1280]{2,1,0:T(8,128)(2,1)}, u32[]{:S(2)}, u32[]{:S(2)}) %all-to-all-start.2) | async-done | bytes 2621472 | tf_op jit(solution)/shard_map/all_to_all | solution.py:97
  421.0 7.3 %gather_fusion.4 = bf16[768,1280]{1,0:T(8,128)(2,1)} fusion(bf16[1024,1280]{1,0:T(8,128)(2,1)} %bitcast.10, s32[1024]{0:T(1024)S(1)} %pad_clamp_fusion), kind=kCustom, calls=%fused_computation.4 | custom fusion | bytes 3935232 | tf_op jit(solution)/shard_map/gather | solution.py:101
  (114 shorter events, 96.2 us)
Async XLA Ops:
  7.2 191.8 %copy-start = (bf16[1,768,1280]{2,1,0:T(8,128)(2,1)S(1)}, bf16[1,768,1280]{2,1,0:T(8,128)(2,1)}, u32[]{:S(2)}) copy-start(bf16[1,768,1280]{2,1,0:T(8,128)(2,1)} %param.13) | copy-start | bytes 5898244
  26.8 27.9 %collective-permute-start = (bf16[1,64,1280]{2,1,0:T(8,128)(2,1)}, bf16[1,64,1280]{2,1,0:T(8,128)(2,1)}, u32[]{:S(2)}, u32[]{:S(2)}) collective-permute-start(bf16[1,64,1280]{2,1,0:T(8,128)(2,1)} %get-tuple-element.19), channel_id=1, source_target_pairs={{0,15},{1,0},{2,1},{3,2},{4,3},{5,4},{6,5},{7,6},{8,7},{9,8},{10,9... | collective-permute-start | bytes 491528 | tf_op jit(solution)/shard_map/ppermute | solution.py:65
  42.2 120.8 %copy-start.8 = (bf16[1,64,1280]{2,1,0:T(8,128)(2,1)S(1)}, bf16[1,64,1280]{2,1,0:T(8,128)(2,1)}, u32[]{:S(2)}) copy-start(bf16[1,64,1280]{2,1,0:T(8,128)(2,1)} %get-tuple-element.11) | copy-start | bytes 491524
  42.2 156.8 %all-to-all-start.1 = ((bf16[16,64,1280]{2,1,0:T(8,128)(2,1)}), bf16[16,64,1280]{2,1,0:T(8,128)(2,1)}, u32[]{:S(2)}, u32[]{:S(2)}) async-start(bf16[16,64,1280]{2,1,0:T(8,128)(2,1)} %fusion), calls=%async_computation.1 | async-start | bytes 5242880 | tf_op jit(solution)/shard_map/all_to_all | solution.py:80
  50.7 176.9 %reduce-scatter.7.cloned.1.call-start = ((), (), s32[]{:S(2)}) async-start(), calls=%async_computation.7 | async-start | bytes 2359296
  50.7 140.0 %collective-permute-start.14 = (bf16[1,64,1280]{2,1,0:T(8,128)(2,1)S(1)}, bf16[1,64,1280]{2,1,0:T(8,128)(2,1)}, u32[]{:S(2)}, u32[]{:S(2)}) collective-permute-start(bf16[1,64,1280]{2,1,0:T(8,128)(2,1)S(1)} %get-tuple-element.5), channel_id=1, source_target_pairs={{0,1},{1,2},{2,3},{3,4},{4,5},{5,6},{6,7},{7,8},{8,9},{9,10},{10,1... | collective-permute-start | bytes 491528 | tf_op jit(solution)/shard_map/ppermute | solution.py:65
  52.3 137.5 %collective-permute-start.13 = (bf16[1,64,1280]{2,1,0:T(8,128)(2,1)S(1)}, bf16[1,64,1280]{2,1,0:T(8,128)(2,1)}, u32[]{:S(2)}, u32[]{:S(2)}) collective-permute-start(bf16[1,64,1280]{2,1,0:T(8,128)(2,1)S(1)} %get-tuple-element.6), channel_id=1, source_target_pairs={{0,2},{1,3},{2,4},{3,5},{4,6},{5,7},{6,8},{7,9},{8,10},{9,11},{10,... | collective-permute-start | bytes 491528 | tf_op jit(solution)/shard_map/ppermute | solution.py:65
  53.5 135.4 %collective-permute-start.12 = (bf16[1,64,1280]{2,1,0:T(8,128)(2,1)S(1)}, bf16[1,64,1280]{2,1,0:T(8,128)(2,1)}, u32[]{:S(2)}, u32[]{:S(2)}) collective-permute-start(bf16[1,64,1280]{2,1,0:T(8,128)(2,1)S(1)} %get-tuple-element.7), channel_id=1, source_target_pairs={{0,3},{1,4},{2,5},{3,6},{4,7},{5,8},{6,9},{7,10},{8,11},{9,12},{10... | collective-permute-start | bytes 491528 | tf_op jit(solution)/shard_map/ppermute | solution.py:65
  53.9 134.0 %collective-permute-start.11 = (bf16[1,64,1280]{2,1,0:T(8,128)(2,1)S(1)}, bf16[1,64,1280]{2,1,0:T(8,128)(2,1)}, u32[]{:S(2)}, u32[]{:S(2)}) collective-permute-start(bf16[1,64,1280]{2,1,0:T(8,128)(2,1)S(1)} %get-tuple-element.8), channel_id=1, source_target_pairs={{0,4},{1,5},{2,6},{3,7},{4,8},{5,9},{6,10},{7,11},{8,12},{9,13},{1... | collective-permute-start | bytes 491528 | tf_op jit(solution)/shard_map/ppermute | solution.py:65
  54.7 63.2 %collective-permute-start.1 = (bf16[1,64,1280]{2,1,0:T(8,128)(2,1)}, bf16[1,64,1280]{2,1,0:T(8,128)(2,1)S(1)}, u32[]{:S(2)}, u32[]{:S(2)}) collective-permute-start(bf16[1,64,1280]{2,1,0:T(8,128)(2,1)} %get-tuple-element.18), channel_id=1, source_target_pairs={{0,14},{1,15},{2,0},{3,1},{4,2},{5,3},{6,4},{7,5},{8,6},{9,7},{10,... | collective-permute-start | bytes 491528 | tf_op jit(solution)/shard_map/ppermute | solution.py:65
  117.9 5.8 %collective-permute-start.2 = (bf16[1,64,1280]{2,1,0:T(8,128)(2,1)}, bf16[1,64,1280]{2,1,0:T(8,128)(2,1)S(1)}, u32[]{:S(2)}, u32[]{:S(2)}) collective-permute-start(bf16[1,64,1280]{2,1,0:T(8,128)(2,1)} %get-tuple-element.17), channel_id=1, source_target_pairs={{0,13},{1,14},{2,15},{3,0},{4,1},{5,2},{6,3},{7,4},{8,5},{9,6},{10... | collective-permute-start | bytes 491528 | tf_op jit(solution)/shard_map/ppermute | solution.py:65
  123.7 4.9 %collective-permute-start.3 = (bf16[1,64,1280]{2,1,0:T(8,128)(2,1)}, bf16[1,64,1280]{2,1,0:T(8,128)(2,1)S(1)}, u32[]{:S(2)}, u32[]{:S(2)}) collective-permute-start(bf16[1,64,1280]{2,1,0:T(8,128)(2,1)} %get-tuple-element.16), channel_id=1, source_target_pairs={{0,12},{1,13},{2,14},{3,15},{4,0},{5,1},{6,2},{7,3},{8,4},{9,5},{1... | collective-permute-start | bytes 491528 | tf_op jit(solution)/shard_map/ppermute | solution.py:65
  128.6 7.7 %collective-permute-start.4 = (bf16[1,64,1280]{2,1,0:T(8,128)(2,1)}, bf16[1,64,1280]{2,1,0:T(8,128)(2,1)S(1)}, u32[]{:S(2)}, u32[]{:S(2)}) collective-permute-start(bf16[1,64,1280]{2,1,0:T(8,128)(2,1)} %get-tuple-element.15), channel_id=1, source_target_pairs={{0,11},{1,12},{2,13},{3,14},{4,15},{5,0},{6,1},{7,2},{8,3},{9,4},{... | collective-permute-start | bytes 491528 | tf_op jit(solution)/shard_map/ppermute | solution.py:65
  136.3 7.6 %collective-permute-start.5 = (bf16[1,64,1280]{2,1,0:T(8,128)(2,1)}, bf16[1,64,1280]{2,1,0:T(8,128)(2,1)S(1)}, u32[]{:S(2)}, u32[]{:S(2)}) collective-permute-start(bf16[1,64,1280]{2,1,0:T(8,128)(2,1)} %get-tuple-element.14), channel_id=1, source_target_pairs={{0,10},{1,11},{2,12},{3,13},{4,14},{5,15},{6,0},{7,1},{8,2},{9,3},... | collective-permute-start | bytes 491528 | tf_op jit(solution)/shard_map/ppermute | solution.py:65
  144.0 6.5 %collective-permute-start.6 = (bf16[1,64,1280]{2,1,0:T(8,128)(2,1)S(1)}, bf16[1,64,1280]{2,1,0:T(8,128)(2,1)S(1)}, u32[]{:S(2)}, u32[]{:S(2)}) collective-permute-start(bf16[1,64,1280]{2,1,0:T(8,128)(2,1)S(1)} %copy-done.10), channel_id=1, source_target_pairs={{0,9},{1,10},{2,11},{3,12},{4,13},{5,14},{6,15},{7,0},{8,1},{9,2},... | collective-permute-start | bytes 491528 | tf_op jit(solution)/shard_map/ppermute | solution.py:65
  150.5 12.5 %collective-permute-start.7 = (bf16[1,64,1280]{2,1,0:T(8,128)(2,1)S(1)}, bf16[1,64,1280]{2,1,0:T(8,128)(2,1)S(1)}, u32[]{:S(2)}, u32[]{:S(2)}) collective-permute-start(bf16[1,64,1280]{2,1,0:T(8,128)(2,1)S(1)} %copy-done.9), channel_id=1, source_target_pairs={{0,8},{1,9},{2,10},{3,11},{4,12},{5,13},{6,14},{7,15},{8,0},{9,1},... | collective-permute-start | bytes 491528 | tf_op jit(solution)/shard_map/ppermute | solution.py:65
  163.0 8.1 %collective-permute-start.8 = (bf16[1,64,1280]{2,1,0:T(8,128)(2,1)S(1)}, bf16[1,64,1280]{2,1,0:T(8,128)(2,1)S(1)}, u32[]{:S(2)}, u32[]{:S(2)}) collective-permute-start(bf16[1,64,1280]{2,1,0:T(8,128)(2,1)S(1)} %copy-done.8), channel_id=1, source_target_pairs={{0,7},{1,8},{2,9},{3,10},{4,11},{5,12},{6,13},{7,14},{8,15},{9,0},... | collective-permute-start | bytes 491528 | tf_op jit(solution)/shard_map/ppermute | solution.py:65
  171.1 8.9 %collective-permute-start.9 = (bf16[1,64,1280]{2,1,0:T(8,128)(2,1)S(1)}, bf16[1,64,1280]{2,1,0:T(8,128)(2,1)S(1)}, u32[]{:S(2)}, u32[]{:S(2)}) collective-permute-start(bf16[1,64,1280]{2,1,0:T(8,128)(2,1)S(1)} %copy-done.7), channel_id=1, source_target_pairs={{0,6},{1,7},{2,8},{3,9},{4,10},{5,11},{6,12},{7,13},{8,14},{9,15},... | collective-permute-start | bytes 491528 | tf_op jit(solution)/shard_map/ppermute | solution.py:65
  180.0 7.9 %collective-permute-start.10 = (bf16[1,64,1280]{2,1,0:T(8,128)(2,1)S(1)}, bf16[1,64,1280]{2,1,0:T(8,128)(2,1)S(1)}, u32[]{:S(2)}, u32[]{:S(2)}) collective-permute-start(bf16[1,64,1280]{2,1,0:T(8,128)(2,1)S(1)} %get-tuple-element.9), channel_id=1, source_target_pairs={{0,5},{1,6},{2,7},{3,8},{4,9},{5,10},{6,11},{7,12},{8,13},{9,14},{... | collective-permute-start | bytes 491528 | tf_op jit(solution)/shard_map/ppermute | solution.py:65
  198.9 57.6 %reduce-scatter.9.cloned.1.call-start = ((), (), s32[]{:S(2)}) async-start(), calls=%async_computation.8 | async-start | bytes 2359296
  204.6 82.6 %all-gather.3.cloned.1.call-start = ((), (), s32[]{:S(2)}) async-start(), calls=%async_computation.5 | async-start | bytes 2359296 | tf_op jit(solution)/shard_map/all_gather | solution.py:18
  292.3 65.2 %all-to-all-start = ((bf16[16,64,1280]{2,1,0:T(8,128)(2,1)}), bf16[16,64,1280]{2,1,0:T(8,128)(2,1)S(1)}, u32[]{:S(2)}, u32[]{:S(2)}) async-start(bf16[16,64,1280]{2,1,0:T(8,128)(2,1)} %bitcast.65), calls=%async_computation | async-start | bytes 5242880 | tf_op jit(solution)/shard_map/all_to_all | solution.py:79
  298.8 29.3 %all-gather.5.cloned.1.call-start = ((), (), s32[]{:S(2)}) async-start(), calls=%async_computation.6 | async-start | bytes 2359296 | tf_op jit(solution)/shard_map/all_gather | solution.py:29
  357.5 63.5 %all-to-all-start.2 = ((bf16[16,64,1280]{2,1,0:T(8,128)(2,1)}), bf16[16,64,1280]{2,1,0:T(8,128)(2,1)}, u32[]{:S(2)}, u32[]{:S(2)}) async-start(bf16[16,64,1280]{2,1,0:T(8,128)(2,1)} %bitcast.66), calls=%async_computation.2 | async-start | bytes 5242880 | tf_op jit(solution)/shard_map/all_to_all | solution.py:97
  (12 other events, 364.6 us)
Sparse Core Ops, SparseCore 0:
  199.1 28.4 reduce-scatter.6
  230.4 26.1 reduce-scatter.8
  260.1 27.1 all-gather.2
  301.5 26.6 all-gather.4
